TPU v7x, 32 devices: a whole 2x2x4 slice. The times are simulated.
32 devices in a mesh: dp: 4 (over x, core), mp: 8 (over z, y).
Axes of the slice: x: 2, y: 2, z: 4, core: 2. Of those that a mesh axis runs over, the one named last changes fastest.
Arguments:
- source_prompts: bfloat16 [128, 64, 4096], P(None, None, 'mp'), may hold values from -6 to 6
- task_logits: float32 [8, 128], replicated, may hold values from -8 to 260
- task_ids: int32 [32], P('dp'), may hold values from 0 to 7
- key_weight: bfloat16 [4096, 4096], P(None, 'mp'), may hold values from -0.09375 to 0.09375
- value_weight: bfloat16 [4096, 4096], P(None, 'mp'), may hold values from -0.09375 to 0.09375
- queries: bfloat16 [32, 128, 4096], P(('dp', 'mp')), may hold values from -32 to 32
- keys: bfloat16 [32, 128, 4096], P(('dp', 'mp')), may hold values from -16 to 16
- values: bfloat16 [32, 128, 4096], P(('dp', 'mp')), may hold values from -6 to 6
- cotangent: bfloat16 [32, 128, 4096], P(('dp', 'mp')), may hold values from -6 to 6
Outputs:
- attended: bfloat16 [32, 128, 4096], P(('dp', 'mp'))
- source_grad: float32 [128, 64, 4096], P(None, 'dp', 'mp')
- logits_grad: float32 [8, 128], replicated
All inputs are finite; a program needn't handle non-finite values.
Results may differ from a plain program's by a relative error of at most 0.011.
Values may be sent and summed in bfloat16 or wider, within the bound.
A program may use at most 128 MiB of HBM per device.

v0:
```python
import jax
import jax.numpy as jnp
from jax import lax
from jax.sharding import PartitionSpec as P

D = 4096
HEADS = 32
DH = 128
NSRC = 128
NTASK = 8
PTOK = 64
SEQ = 128
E_DEV = 1
mask_fill = -1e30


def example_block(prompt_pair, queries, keys, values, cotangent):
    examples = queries.shape[0]
    score_scale = DH ** (-0.5)
    key_all = jnp.concatenate([prompt_pair[:, :, 0, :], keys], axis=1)
    value_all = jnp.concatenate([prompt_pair[:, :, 1, :], values], axis=1)
    query_heads = queries.reshape(examples, SEQ, HEADS, DH)
    key_heads = key_all.reshape(examples, PTOK + SEQ, HEADS, DH)
    value_heads = value_all.reshape(examples, PTOK + SEQ, HEADS, DH)
    cot_heads = cotangent.reshape(examples, SEQ, HEADS, DH)
    scores = (
        jnp.einsum("eihd,ejhd->ehij", query_heads, key_heads, preferred_element_type=jnp.float32)
        * score_scale
    )
    column = jnp.arange(PTOK + SEQ)[None, :]
    position = jnp.arange(SEQ)[:, None]
    visible = (column < PTOK) | (column - PTOK <= position)
    scores = jnp.where(visible[None, None], scores, mask_fill)
    top_score = jnp.max(scores, axis=3, keepdims=True)
    exponent = jnp.exp(scores - top_score)
    attention = exponent / jnp.sum(exponent, axis=3, keepdims=True)
    attention_rounded = attention.astype(jnp.bfloat16)
    attended = jnp.einsum(
        "ehij,ejhd->eihd", attention_rounded, value_heads, preferred_element_type=jnp.float32
    )
    attended = attended.astype(jnp.bfloat16).reshape(examples, SEQ, D)
    grad_attention = jnp.einsum(
        "eihd,ejhd->ehij", cot_heads, value_heads, preferred_element_type=jnp.float32
    )
    inner_sum = jnp.sum(attention * grad_attention, axis=3, keepdims=True)
    grad_scores = (attention * (grad_attention - inner_sum)).astype(jnp.bfloat16)
    key_grads = jnp.einsum(
        "ehij,eihd->ejhd",
        grad_scores[:, :, :, :PTOK],
        query_heads,
        preferred_element_type=jnp.float32,
    )
    key_grads = (key_grads * score_scale).astype(jnp.bfloat16).reshape(examples, PTOK, D)
    value_grads = jnp.einsum(
        "ehij,eihd->ejhd",
        attention_rounded[:, :, :, :PTOK],
        cot_heads,
        preferred_element_type=jnp.float32,
    )
    value_grads = value_grads.astype(jnp.bfloat16).reshape(examples, PTOK, D)
    return (attended, jnp.stack([key_grads, value_grads], axis=2))


def tile_products(tile_grad, source_prompts, mix_weights, col_width):
    rows_here = tile_grad.shape[1]
    own_prompts = lax.dynamic_slice_in_dim(
        source_prompts, lax.axis_index("dp") * rows_here, rows_here, 1
    )
    tile_flat = tile_grad.reshape(NTASK, rows_here * col_width)
    source_grad = jnp.dot(mix_weights.T, tile_flat, precision=lax.Precision.HIGHEST)
    source_grad = source_grad.reshape(NSRC, rows_here, col_width)
    weight_part = jnp.dot(
        tile_flat,
        own_prompts.reshape(NSRC, rows_here * col_width).astype(jnp.float32).T,
        precision=lax.Precision.HIGHEST,
    )
    return (source_grad, weight_part)


def on_device(
    source_prompts,
    task_logits,
    task_ids,
    key_weight,
    value_weight,
    queries,
    keys,
    values,
    cotangent,
):
    col_width = key_weight.shape[1]
    group_examples = task_ids.shape[0]
    mix_weights = jax.nn.softmax(task_logits, axis=1)
    mix_rounded = mix_weights.astype(jnp.bfloat16)
    mixture = jnp.dot(
        mix_rounded,
        source_prompts.reshape(NSRC, PTOK * col_width),
        preferred_element_type=jnp.float32,
    )
    mixture = mixture.astype(jnp.bfloat16).reshape(NTASK, PTOK, col_width)
    pair_weight = jnp.concatenate([key_weight, value_weight], axis=1)
    portion = lax.all_gather(mixture, "mp", axis=2, tiled=True)
    portion_rows = portion.reshape(NTASK * PTOK, portion.shape[2])
    projected = jnp.dot(portion_rows, pair_weight, preferred_element_type=jnp.float32)
    projected = projected.astype(jnp.bfloat16).reshape(NTASK, PTOK, 2, col_width)
    task_range = jnp.arange(NTASK, dtype=jnp.int32)
    selector_all = (task_ids[:, None] == task_range[None, :]).astype(jnp.bfloat16)
    table_full = lax.all_gather(projected, "mp", axis=3, tiled=True)
    own_offset = lax.axis_index("mp") * E_DEV
    own_selector = lax.dynamic_slice_in_dim(selector_all, own_offset, E_DEV, 0)
    chosen = jnp.dot(
        own_selector, table_full.reshape(NTASK, PTOK * 2 * D), preferred_element_type=jnp.float32
    )
    prompt_pair = chosen.astype(jnp.bfloat16).reshape(E_DEV, PTOK, 2, D)
    attended, outgoing_grads = example_block(prompt_pair, queries, keys, values, cotangent)
    incoming = lax.all_to_all(outgoing_grads, "mp", split_axis=3, concat_axis=0, tiled=True)
    group_grads = jnp.dot(
        selector_all.T,
        incoming.reshape(group_examples, PTOK * 2 * col_width),
        preferred_element_type=jnp.float32,
    )
    pair_weight_t = pair_weight.astype(jnp.float32).T
    task_rows = lax.psum_scatter(
        group_grads.reshape(NTASK, PTOK, 2 * col_width), "dp", scatter_dimension=1, tiled=True
    )
    rows_here = task_rows.shape[1]
    row_terms = jnp.dot(
        task_rows.reshape(NTASK * rows_here, 2 * col_width),
        pair_weight_t,
        precision=lax.Precision.HIGHEST,
    ).reshape(NTASK, rows_here, D)
    tile_grad = lax.psum_scatter(row_terms, "mp", scatter_dimension=2, tiled=True)
    source_grad, weight_part = tile_products(tile_grad, source_prompts, mix_weights, col_width)
    weight_grad = lax.psum(weight_part, ("dp", "mp"))
    logits_grad = mix_weights * (
        weight_grad - jnp.sum(mix_weights * weight_grad, axis=1, keepdims=True)
    )
    return (attended, source_grad, logits_grad)


def solution(mesh):
    placed = (
        P(None, None, "mp"),
        P(),
        P("dp"),
        P(None, "mp"),
        P(None, "mp"),
        P(("dp", "mp"), None, None),
        P(("dp", "mp"), None, None),
        P(("dp", "mp"), None, None),
        P(("dp", "mp"), None, None),
    )
    return jax.shard_map(
        on_device,
        mesh=mesh,
        in_specs=placed,
        out_specs=(P(("dp", "mp"), None, None), P(None, "dp", "mp"), P()),
        check_vma=False,
    )
```

profile of v0, /device:TPU:0, one launch (start us, length us, event | category | flops | bytes accessed | tf_op | source)
XLA Modules:
  0.0 497.0 jit_solution(17414920822181697347)
XLA Ops:
  7.2 0.8 reduce_max.18
  8.0 0.9 fusion.44
  8.9 12.5 %copy.91 = bf16[16,8,64,512]{3,1,2,0:T(8,128)(2,1)} copy(bf16[16,8,64,512]{3,2,1,0:T(8,128)(2,1)} %bitcast.125) | data formatting | bytes 16777216
  21.4 4.6 convolution_convert_fusion
  26.0 1.0 copy.63
  27.0 4.7 constant_dynamic-update-slice_fusion.1
  31.7 2.3 constant_dynamic-update-slice_fusion
  34.0 70.5 %all-gather.3.cloned.1.call-done = bf16[8,64,4096]{2,1,0:T(8,128)(2,1)} async-done(((bf16[8,64,512]{2,1,0:T(8,128)(2,1)}), bf16[8,64,4096]{2,1,0:T(8,128)(2,1)}) %all-gather.3.cloned.1.call-update) | async-done | bytes 4194320 | tf_op jit(solution)/shard_map/all_gather | solution.py:102
  104.5 9.1 %convolution_convert_fusion.1 = bf16[512,1024]{1,0:T(8,128)(2,1)S(1)} fusion(bf16[512,4096]{1,0:T(8,128)(2,1)} %bitcast.147, bf16[4096,1024]{1,0:T(8,128)(2,1)} %constant_dynamic-update-slice_fusion), kind=kOutput, calls=%fused_computation.30 | convolution fusion | flops 4295491584 | bytes 13631488 | tf_op jit(solution)/shard_map/dot_general | solution.py:104
  113.7 1.6 reshape.180
  115.3 0.2 reduce-scatter.3.cloned.1.call-start
  115.5 1.2 copy.94
  116.7 0.7 copy.67
  117.4 1.3 copy.69
  118.7 0.7 copy.64
  119.3 1.4 copy.73
  120.7 1.6 copy.95
  122.4 0.1 fusion.38
  122.5 116.0 %all-gather.5.cloned.1.call-done = bf16[8,64,2,4096]{3,2,1,0:T(2,128)(2,1)} async-done(((bf16[8,64,2,512]{3,2,1,0:T(2,128)(2,1)}), bf16[8,64,2,4096]{3,2,1,0:T(2,128)(2,1)}) %all-gather.5.cloned.1.call-update) | async-done | bytes 8388624 | tf_op jit(solution)/shard_map/all_gather | solution.py:108
  238.5 13.0 %reshape.181 = bf16[8,524288]{1,0:T(8,128)(2,1)} reshape(bf16[8,64,2,4096]{3,2,1,0:T(2,128)(2,1)} %all-gather.5.cloned.1.call-done) | data formatting | bytes 16777216 | tf_op jit(solution)/shard_map/reshape | solution.py:112
  251.5 5.7 %fusion.46 = f32[1,524288]{1,0:T(1,128)S(1)} fusion(bf16[8,524288]{1,0:T(8,128)(2,1)} %reshape.181, pred[8,8]{1,0:T(8,128)(4,1)S(1)} %iota_compare_fusion.1, s32[]{:T(128)S(6)} %select_n.11), kind=kOutput, calls=%fused_computation.69 | convolution fusion | flops 8388608 | bytes 10486276 | tf_op jit(solution)/shard_map/dot_general | solution.py:111
  257.2 1.1 convert_element_type.64
  258.3 1.3 reshape.182
  259.7 5.6 %slice_reduce_fusion = (bf16[64,4096]{1,0:T(8,128)(2,1)S(1)}, bf16[64,4096]{1,0:T(8,128)(2,1)S(1)}) fusion(bf16[1,64,2,4096]{3,2,1,0:T(2,128)(2,1)S(1)} %reshape.182), kind=kLoop, calls=%fused_computation.40 | loop fusion | bytes 2097152 | tf_op jit(solution)/shard_map/slice | solution.py:20
  265.4 0.2 copy.68
  265.6 0.1 copy_bitcast_fusion
  265.8 0.8 fusion.12
  266.6 0.9 fusion.57
  267.5 1.5 convert_bitcast_fusion
  269.0 0.5 copy-done.4
  269.5 0.9 fusion.15
  270.4 0.8 fusion.22
  271.2 0.6 fusion.27
  271.7 0.3 copy.76
  272.1 0.2 stack_reshape.6
  272.3 1.6 fusion.26
  273.9 0.3 copy.78
  274.3 0.2 stack_reshape.7
  274.5 1.1 pad_maximum_fusion
  275.6 5.0 %copy.79 = bf16[1,64,2,4096]{1,2,0,3:T(2,128)(2,1)S(1)} copy(bf16[1,64,2,4096]{3,1,2,0:T(8,128)(2,1)} %pad_maximum_fusion) | data formatting | bytes 2097152 | tf_op jit(solution)/shard_map/stack | solution.py:61
  280.6 2.7 reshape.201
  283.3 29.5 %all_to_all.15 = bf16[8,2,32768]{2,1,0:T(2,128)(2,1)} all-to-all(bf16[8,2,32768]{2,1,0:T(2,128)(2,1)} %reshape.201), channel_id=1, replica_groups=mesh['dp'=4,'mp'=8] {'mp'}, dimensions={0} | all-to-all | bytes 2097152 | tf_op jit(solution)/shard_map/all_to_all | solution.py:116
  312.8 3.1 reshape.202
  315.9 3.6 copy.80
  319.5 2.0 reshape.190
  321.6 1.9 fusion.41
  323.5 0.4 reduce-scatter.5.cloned.1.call-start
  323.9 29.9 %reduce-scatter.3.cloned.1.call-done = f32[8,16,1024]{2,0,1:T(8,128)} async-done(((f32[8,64,1024]{2,0,1:T(8,128)}), f32[8,16,1024]{2,0,1:T(8,128)}) %reduce-scatter.3.cloned.1.call-update) | async-done | bytes 524304 | tf_op jit(solution)/shard_map/reduce_scatter | solution.py:123
  353.8 13.3 %fusion.2 = f32[8,16,4096]{2,1,0:T(8,128)} fusion(bf16[4096,1024]{1,0:T(8,128)(2,1)} %constant_dynamic-update-slice_fusion, f32[8,16,1024]{2,0,1:T(8,128)} %reduce-scatter.3.cloned.1.call-done), kind=kOutput, calls=%fused_computation.3 | convolution fusion | flops 6442450944 | bytes 11010048 | tf_op jit(solution)/shard_map/dot_general | solution.py:127
  367.2 1.3 copy.66
  368.5 1.9 constant_dynamic-slice_fusion
  370.4 0.1 copy.92
  370.5 0.2 copy.65
  370.8 0.4 copy-done.7
  371.2 0.3 copy-done.11
  371.5 0.8 fusion.23
  372.3 1.3 copy.85
  373.6 62.5 %reduce-scatter.5.cloned.1.call-done = f32[8,16,512]{2,1,0:T(8,128)} async-done(((f32[8,16,4096]{2,1,0:T(8,128)}), f32[8,16,512]{2,1,0:T(8,128)}) %reduce-scatter.5.cloned.1.call-update) | async-done | bytes 262160 | tf_op jit(solution)/shard_map/reduce_scatter | solution.py:132
  436.2 4.6 fusion.28
  440.8 39.7 %psum.7 = f32[8,128]{1,0:T(8,128)S(1)} all-reduce(f32[8,128]{1,0:T(8,128)S(1)} %fusion.28), channel_id=1, replica_groups=mesh['dp'=4,'mp'=8] {'dp','mp'}, use_global_device_ids=true, to_apply=%region_7.8 | all-reduce | flops 1024 | bytes 8192 | tf_op jit(solution)/shard_map/psum | solution.py:134
  480.5 0.2 multiply_reduce_fusion
  480.7 0.7 subtract_multiply_fusion
  481.4 4.5 fusion.39
  485.9 4.4 copy.86
  (35 shorter events, 0.4 us)
Async XLA Ops:
  7.2 97.3 %all-gather.3.cloned.1.call-start = ((), (), s32[]{:S(2)}) async-start(), calls=%async_computation.3 | async-start | bytes 4718592 | tf_op jit(solution)/shard_map/all_gather | solution.py:102
  8.9 12.5 %copy-start.12 = (f32[8,128]{1,0:T(8,128)S(1)}, f32[8,128]{1,0:T(8,128)}, u32[]{:S(2)}) copy-start(f32[8,128]{1,0:T(8,128)} %param.10) | copy-start | bytes 12292
  27.0 211.6 %all-gather.5.cloned.1.call-start = ((), (), s32[]{:S(2)}) async-start(), calls=%async_computation.4 | async-start | bytes 9437184 | tf_op jit(solution)/shard_map/all_gather | solution.py:108
  27.0 4.7 copy-start.2
  113.6 1.9 copy-start.8
  113.6 3.1 copy-start.9
  115.3 238.6 %reduce-scatter.3.cloned.1.call-start = ((), (), s32[]{:S(2)}) async-start(), calls=%async_computation.5 | async-start | bytes 2621440 | tf_op jit(solution)/shard_map/reduce_scatter | solution.py:123
  115.5 3.2 copy-start.10
  118.7 3.7 copy-start.13
  259.6 6.1 %copy-start.3 = (bf16[16,8,32,128]{3,2,1,0:T(8,128)(2,1)S(1)}, bf16[16,8,32,128]{3,2,1,0:T(8,128)(2,1)}, u32[]{:S(2)}) copy-start(bf16[16,8,32,128]{3,2,1,0:T(8,128)(2,1)} %copy.94) | copy-start | bytes 3145732
  259.6 6.1 %copy-start.5 = (bf16[1,128,32,128]{3,1,2,0:T(8,128)(2,1)S(1)}, bf16[1,128,32,128]{3,1,2,0:T(8,128)(2,1)}, u32[]{:S(2)}) copy-start(bf16[1,128,32,128]{3,1,2,0:T(8,128)(2,1)} %copy.69) | copy-start | bytes 3145732
  265.3 1.3 copy-start
  267.5 2.9 copy-start.6
  267.5 2.0 copy-start.4
  323.5 112.7 %reduce-scatter.5.cloned.1.call-start = ((), (), s32[]{:S(2)}) async-start(), calls=%async_computation.6 | async-start | bytes 2359296 | tf_op jit(solution)/shard_map/reduce_scatter | solution.py:132
  368.5 1.9 copy-start.1
  368.5 2.7 copy-start.7
  368.5 3.0 copy-start.11
Sparse Core Ops, SparseCore 0:
  27.1 77.3 all-gather.2
  115.4 123.1 all-gather.4
  323.6 30.1 reduce-scatter.2
  367.3 68.8 reduce-scatter.4
where the time goes:
time: 506 us; the launch traced here: 497 us
  waiting for transfers between devices  279 us (55%)
  local copies, waits for them, and re-layouts  77.2 us (15%)
  blocking collectives  69.3 us (14%)
  matrix products  48.5 us (10%)
  between operations  14.3 us (3%)
  other arithmetic  8.09 us (2%)
    all_gather x1, waiting for transfers between devices, on_device(): table_full = lax.all_gather(projected, 'mp', axis=3, tiled=True)  116 us
    all_gather x1, waiting for transfers between devices, on_device(): portion = lax.all_gather(mixture, 'mp', axis=2, tiled=True)  70.5 us
    reduce_scatter x1, waiting for transfers between devices, on_device(): lax.psum_scatter(row_terms, 'mp', scatter_dimension=2, tiled=True)  62.5 us
    psum x1, blocking collectives, on_device(): weight_grad = lax.psum(weight_part, ('dp', 'mp'))  39.7 us
    unnamed x40, local copies, waits for them, and re-layouts  34.1 us
    reduce_scatter x1, waiting for transfers between devices, on_device(): lax.psum_scatter(group_grads.reshape(NTASK, PTOK, 2 * col_width), 'dp', s...  29.9 us
    all_to_all x1, blocking collectives, on_device(): lax.all_to_all(outgoing_grads, 'mp', split_axis=3, concat_axis=0, tiled=T...  29.5 us
    dot_general x1, matrix products, on_device(): jnp.dot(task_rows.reshape(NTASK * rows_here, 2 * col_width), pair_weight_...  13.3 us
  transfers between devices with their start and end apart: 4, of which 4 were waited for; matrix products, arithmetic and copies ran while one was open for 4% of the time, Pallas kernels for 0%

commit v1 on v0

--- a/solution.py
+++ b/solution.py
@@ -12,6 +12,11 @@
 SEQ = 128
 E_DEV = 1
 mask_fill = -1e30
+
+
+def add_all(shard, axis):
+    blocks = lax.all_gather(shard, axis)
+    return jnp.sum(blocks, axis=0)
 
 
 def example_block(prompt_pair, queries, keys, values, cotangent):
@@ -131,7 +136,7 @@
     ).reshape(NTASK, rows_here, D)
     tile_grad = lax.psum_scatter(row_terms, "mp", scatter_dimension=2, tiled=True)
     source_grad, weight_part = tile_products(tile_grad, source_prompts, mix_weights, col_width)
-    weight_grad = lax.psum(weight_part, ("dp", "mp"))
+    weight_grad = add_all(weight_part, ("dp", "mp"))
     logits_grad = mix_weights * (
         weight_grad - jnp.sum(mix_weights * weight_grad, axis=1, keepdims=True)
     )

time: 506 us -> 532 us (1.051)
  blocking collectives: 69.3 us -> 94.7 us
    all_gather x0 -> x1, blocking collectives: none -> 65.2 us  [add_all(): blocks = lax.all_gather(shard, axis)]
    psum x1 -> x0, blocking collectives: 39.7 us -> none  [on_device(): weight_grad = lax.psum(weight_part, ('dp', 'mp'))]
where the time goes in v1:
time: 532 us; the launch traced here: 522 us
  waiting for transfers between devices  279 us (52%)
  blocking collectives  94.7 us (18%)
  local copies, waits for them, and re-layouts  77.2 us (15%)
  matrix products  48.5 us (9%)
  between operations  14.3 us (3%)
  other arithmetic  8.12 us (2%)
    all_gather x1, waiting for transfers between devices, on_device(): table_full = lax.all_gather(projected, 'mp', axis=3, tiled=True)  116 us
    all_gather x1, waiting for transfers between devices, on_device(): portion = lax.all_gather(mixture, 'mp', axis=2, tiled=True)  70.5 us
    all_gather x1, blocking collectives, add_all(): blocks = lax.all_gather(shard, axis)  65.2 us
    reduce_scatter x1, waiting for transfers between devices, on_device(): lax.psum_scatter(row_terms, 'mp', scatter_dimension=2, tiled=True)  62.5 us
    unnamed x40, local copies, waits for them, and re-layouts  34.1 us
    reduce_scatter x1, waiting for transfers between devices, on_device(): lax.psum_scatter(group_grads.reshape(NTASK, PTOK, 2 * col_width), 'dp', s...  29.9 us
    all_to_all x1, blocking collectives, on_device(): lax.all_to_all(outgoing_grads, 'mp', split_axis=3, concat_axis=0, tiled=T...  29.5 us
    dot_general x1, matrix products, on_device(): jnp.dot(task_rows.reshape(NTASK * rows_here, 2 * col_width), pair_weight_...  13.3 us
  transfers between devices with their start and end apart: 4, of which 4 were waited for; matrix products, arithmetic and copies ran while one was open for 4% of the time, Pallas kernels for 0%

profile of v1, /device:TPU:0, one launch (start us, length us, event | category | flops | bytes accessed | tf_op | source)
XLA Modules:
  0.0 522.5 jit_solution(756910834729387383)
XLA Ops:
  7.2 0.8 reduce_max.18
  8.0 0.9 fusion.44
  8.9 12.5 %copy.91 = bf16[16,8,64,512]{3,1,2,0:T(8,128)(2,1)} copy(bf16[16,8,64,512]{3,2,1,0:T(8,128)(2,1)} %bitcast.127) | data formatting | bytes 16777216
  21.4 4.6 convolution_convert_fusion
  26.0 1.0 copy.63
  27.0 4.7 constant_dynamic-update-slice_fusion.1
  31.7 2.3 constant_dynamic-update-slice_fusion
  34.0 70.5 %all-gather.4.cloned.1.call-done = bf16[8,64,4096]{2,1,0:T(8,128)(2,1)} async-done(((bf16[8,64,512]{2,1,0:T(8,128)(2,1)}), bf16[8,64,4096]{2,1,0:T(8,128)(2,1)}) %all-gather.4.cloned.1.call-update) | async-done | bytes 4194320 | tf_op jit(solution)/shard_map/all_gather | solution.py:107
  104.5 9.1 %convolution_convert_fusion.1 = bf16[512,1024]{1,0:T(8,128)(2,1)S(1)} fusion(bf16[512,4096]{1,0:T(8,128)(2,1)} %bitcast.149, bf16[4096,1024]{1,0:T(8,128)(2,1)} %constant_dynamic-update-slice_fusion), kind=kOutput, calls=%fused_computation.30 | convolution fusion | flops 4295491584 | bytes 13631488 | tf_op jit(solution)/shard_map/dot_general | solution.py:109
  113.7 1.6 reshape.180
  115.3 0.2 reduce-scatter.3.cloned.1.call-start
  115.5 1.2 copy.94
  116.7 0.7 copy.67
  117.4 1.3 copy.69
  118.7 0.7 copy.64
  119.3 1.4 copy.73
  120.7 1.6 copy.95
  122.4 0.1 fusion.38
  122.5 116.0 %all-gather.6.cloned.1.call-done = bf16[8,64,2,4096]{3,2,1,0:T(2,128)(2,1)} async-done(((bf16[8,64,2,512]{3,2,1,0:T(2,128)(2,1)}), bf16[8,64,2,4096]{3,2,1,0:T(2,128)(2,1)}) %all-gather.6.cloned.1.call-update) | async-done | bytes 8388624 | tf_op jit(solution)/shard_map/all_gather | solution.py:113
  238.5 13.0 %reshape.181 = bf16[8,524288]{1,0:T(8,128)(2,1)} reshape(bf16[8,64,2,4096]{3,2,1,0:T(2,128)(2,1)} %all-gather.6.cloned.1.call-done) | data formatting | bytes 16777216 | tf_op jit(solution)/shard_map/reshape | solution.py:117
  251.5 5.7 %fusion.46 = f32[1,524288]{1,0:T(1,128)S(1)} fusion(bf16[8,524288]{1,0:T(8,128)(2,1)} %reshape.181, pred[8,8]{1,0:T(8,128)(4,1)S(1)} %iota_compare_fusion.1, s32[]{:T(128)S(6)} %select_n.11), kind=kOutput, calls=%fused_computation.70 | convolution fusion | flops 8388608 | bytes 10486276 | tf_op jit(solution)/shard_map/dot_general | solution.py:116
  257.2 1.1 convert_element_type.64
  258.3 1.3 reshape.182
  259.7 5.6 %slice_reduce_fusion = (bf16[64,4096]{1,0:T(8,128)(2,1)S(1)}, bf16[64,4096]{1,0:T(8,128)(2,1)S(1)}) fusion(bf16[1,64,2,4096]{3,2,1,0:T(2,128)(2,1)S(1)} %reshape.182), kind=kLoop, calls=%fused_computation.40 | loop fusion | bytes 2097152 | tf_op jit(solution)/shard_map/slice | solution.py:25
  265.4 0.2 copy.68
  265.6 0.1 copy_bitcast_fusion
  265.8 0.8 fusion.12
  266.6 0.9 fusion.57
  267.5 1.5 convert_bitcast_fusion
  269.0 0.5 copy-done.4
  269.5 0.9 fusion.15
  270.4 0.8 fusion.22
  271.2 0.6 fusion.27
  271.7 0.3 copy.76
  272.1 0.2 stack_reshape.6
  272.3 1.6 fusion.26
  273.9 0.3 copy.78
  274.3 0.2 stack_reshape.7
  274.5 1.1 pad_maximum_fusion
  275.6 5.0 copy.79
  280.6 2.7 reshape.202
  283.3 29.5 %all_to_all.15 = bf16[8,2,32768]{2,1,0:T(2,128)(2,1)} all-to-all(bf16[8,2,32768]{2,1,0:T(2,128)(2,1)} %reshape.202), channel_id=1, replica_groups=mesh['dp'=4,'mp'=8] {'mp'}, dimensions={0} | all-to-all | bytes 2097152 | tf_op jit(solution)/shard_map/all_to_all | solution.py:121
  312.8 3.1 reshape.203
  315.9 3.6 copy.80
  319.5 2.0 reshape.190
  321.6 1.9 fusion.41
  323.5 0.4 reduce-scatter.5.cloned.1.call-start
  323.9 29.9 %reduce-scatter.3.cloned.1.call-done = f32[8,16,1024]{2,0,1:T(8,128)} async-done(((f32[8,64,1024]{2,0,1:T(8,128)}), f32[8,16,1024]{2,0,1:T(8,128)}) %reduce-scatter.3.cloned.1.call-update) | async-done | bytes 524304 | tf_op jit(solution)/shard_map/reduce_scatter | solution.py:128
  353.8 13.3 %fusion.2 = f32[8,16,4096]{2,1,0:T(8,128)} fusion(bf16[4096,1024]{1,0:T(8,128)(2,1)} %constant_dynamic-update-slice_fusion, f32[8,16,1024]{2,0,1:T(8,128)} %reduce-scatter.3.cloned.1.call-done), kind=kOutput, calls=%fused_computation.3 | convolution fusion | flops 6442450944 | bytes 11010048 | tf_op jit(solution)/shard_map/dot_general | solution.py:132
  367.2 1.3 copy.66
  368.5 1.9 constant_dynamic-slice_fusion
  370.4 0.1 copy.92
  370.5 0.2 copy.65
  370.8 0.4 copy-done.7
  371.2 0.3 copy-done.11
  371.5 0.8 fusion.23
  372.3 1.3 copy.85
  373.6 62.5 %reduce-scatter.5.cloned.1.call-done = f32[8,16,512]{2,1,0:T(8,128)} async-done(((f32[8,16,4096]{2,1,0:T(8,128)}), f32[8,16,512]{2,1,0:T(8,128)}) %reduce-scatter.5.cloned.1.call-update) | async-done | bytes 262160 | tf_op jit(solution)/shard_map/reduce_scatter | solution.py:137
  436.2 4.6 fusion.28
  440.8 65.2 %all-gather = f32[256,128]{1,0:T(8,128)S(1)} all-gather(f32[8,128]{1,0:T(8,128)S(1)} %fusion.28), channel_id=2, replica_groups=mesh['dp'=4,'mp'=8] {'dp','mp'}, dimensions={0}, use_global_device_ids=true | all-gather | bytes 135168 | tf_op jit(solution)/shard_map/all_gather | solution.py:18
  506.0 0.2 multiply_reduce_fusion
  506.1 0.7 subtract_multiply_fusion
  506.8 4.5 fusion.39
  511.3 4.4 copy.86
  (36 shorter events, 0.4 us)
Async XLA Ops:
  7.2 97.3 %all-gather.4.cloned.1.call-start = ((), (), s32[]{:S(2)}) async-start(), calls=%async_computation.3 | async-start | bytes 4718592 | tf_op jit(solution)/shard_map/all_gather | solution.py:107
  8.9 12.5 %copy-start.12 = (f32[8,128]{1,0:T(8,128)S(1)}, f32[8,128]{1,0:T(8,128)}, u32[]{:S(2)}) copy-start(f32[8,128]{1,0:T(8,128)} %param.10) | copy-start | bytes 12292
  27.0 211.6 %all-gather.6.cloned.1.call-start = ((), (), s32[]{:S(2)}) async-start(), calls=%async_computation.4 | async-start | bytes 9437184 | tf_op jit(solution)/shard_map/all_gather | solution.py:113
  27.0 4.7 copy-start.2
  113.6 1.9 copy-start.8
  113.6 3.1 copy-start.9
  115.3 238.6 %reduce-scatter.3.cloned.1.call-start = ((), (), s32[]{:S(2)}) async-start(), calls=%async_computation.5 | async-start | bytes 2621440 | tf_op jit(solution)/shard_map/reduce_scatter | solution.py:128
  115.5 3.2 copy-start.10
  118.7 3.7 copy-start.13
  259.6 6.1 %copy-start.3 = (bf16[16,8,32,128]{3,2,1,0:T(8,128)(2,1)S(1)}, bf16[16,8,32,128]{3,2,1,0:T(8,128)(2,1)}, u32[]{:S(2)}) copy-start(bf16[16,8,32,128]{3,2,1,0:T(8,128)(2,1)} %copy.94) | copy-start | bytes 3145732
  259.6 6.1 %copy-start.5 = (bf16[1,128,32,128]{3,1,2,0:T(8,128)(2,1)S(1)}, bf16[1,128,32,128]{3,1,2,0:T(8,128)(2,1)}, u32[]{:S(2)}) copy-start(bf16[1,128,32,128]{3,1,2,0:T(8,128)(2,1)} %copy.69) | copy-start | bytes 3145732
  265.3 1.3 copy-start
  267.5 2.9 copy-start.6
  267.5 2.0 copy-start.4
  323.5 112.7 %reduce-scatter.5.cloned.1.call-start = ((), (), s32[]{:S(2)}) async-start(), calls=%async_computation.6 | async-start | bytes 2359296 | tf_op jit(solution)/shard_map/reduce_scatter | solution.py:137
  368.5 1.9 copy-start.1
  368.5 2.7 copy-start.7
  368.5 3.0 copy-start.11
Sparse Core Ops, SparseCore 0:
  27.1 77.3 all-gather.3
  115.4 123.1 all-gather.5
  323.6 30.1 reduce-scatter.2
  367.3 68.8 reduce-scatter.4
